TPU v7x, 32 devices: a whole 2x2x4 slice. The times are simulated.
32 devices in a mesh: gz: 16 (over z, y, x), gy: 2 (over core).
Axes of the slice: x: 2, y: 2, z: 4, core: 2. Of those that a mesh axis runs over, the one named last changes fastest.
Arguments:
- velocity: bfloat16 [3, 128, 128, 128], P(None, 'gz', 'gy'), may hold values from -6 to 6
- palette_color: float32 [3, 64], replicated, may hold values from 0 to 1
- palette_extinction: float32 [64], replicated, may hold values from 0.0003 to 0.02
- palette_index: int32 [16], replicated, may hold values from 0 to 63
Outputs:
- image: float32 [4, 2, 64, 128], P(None, 'gy', 'gz')
All inputs are finite; a program needn't handle non-finite values.
Results may differ from a plain program's by a relative error of at most 0.0012.
Values may be sent and summed in bfloat16 or wider, within the bound.
A program may use at most 64 MiB of HBM per device.

v0:
```python
import functools
import math

import jax
import jax.numpy as jnp
import numpy as np
from jax import lax
from jax.experimental import pallas as pl
from jax.experimental.pallas import tpu as pltpu
from jax.sharding import PartitionSpec as P

RADIUS = 4
TF_POINTS = 16
PAD = 8
BLOCK = 16
EDGE = 4
IN_FLIGHT = 3
MESH = pl.DeviceIdType.MESH

filter_sigma = 1.5
vortex_gain = 400.0


def filter_taps():
    weights = [
        math.exp(-((offset - RADIUS) ** 2) / (2.0 * filter_sigma**2))
        for offset in range(2 * RADIUS + 1)
    ]
    weight_sum = sum(weights)
    gauss = [weight / weight_sum for weight in weights]
    moment = sum(((offset - RADIUS) ** 2 * gauss[offset] for offset in range(2 * RADIUS + 1)))
    deriv = [(offset - RADIUS) * gauss[offset] / moment for offset in range(2 * RADIUS + 1)]
    return (gauss, deriv)


def banded(taps, outs, ins, shift):
    band = np.zeros((outs, ins), np.float64)
    for i in range(outs):
        for offset in range(2 * RADIUS + 1):
            k = i + shift + offset - RADIUS
            if 0 <= k < ins:
                band[i, k] = taps[offset]
    return band


def high_low(band):
    band = band.astype(np.float32)
    high = band.astype(jnp.bfloat16)
    low = (band - high.astype(np.float32)).astype(jnp.bfloat16)
    return high, low


def operators(half, columns):
    gauss, deriv = filter_taps()
    z_of = [banded(taps, half, half + 2 * RADIUS, RADIUS) for taps in (gauss, deriv)]
    y_of = [banded(taps, BLOCK, BLOCK + 2 * PAD, PAD) for taps in (gauss, deriv)]
    both = np.concatenate([np.kron(z_of[0], y_of[0]), np.kron(z_of[0], y_of[1]), np.kron(z_of[1], y_of[0])], 0)
    depth_rows = np.concatenate(high_low(both), 0)
    across = []
    for taps in (deriv, gauss):
        high, low = high_low(banded(taps, columns, columns, 0).T)
        across.append(np.block([[high, low], [high, np.zeros_like(low)]]))
    return depth_rows, np.stack(across)


def transfers(rows, n_gy):
    blocks = rows // BLOCK
    ends = [min(rows, (block + 1) * BLOCK + PAD) for block in range(blocks)]
    edges = [(1, rows - EDGE, PAD - EDGE, EDGE, 0), (-1, 0, PAD + rows, EDGE, blocks - 1)] if n_gy > 1 else []
    sides = [(1, rows - PAD, 0, PAD, 0), (-1, 0, PAD + rows, PAD, blocks - 1)] if n_gy > 1 else []
    moves = [(0, *side) for side in sides]
    for dz in (1, -1):
        start = 0
        for block, end in enumerate(ends):
            moves += [(dz, *edge) for edge in edges if edge[-1] == block]
            if end > start:
                moves.append((dz, 0, start, PAD + start, end - start, block))
            start = end
    return moves


def kernel(
    n, n_gy, velocity, depth_hbm, across_hbm, color_hbm, extinction_hbm, index_hbm, out,
    brick, depth_rows, across, color, extinction, index, table, front, staged, sent, got,
    local_sem, halo_send, halo_got, piece_send, piece_got, heard,
):
    parts, depth, rows, columns = velocity.shape
    half = depth // 2
    group = rows // n
    me, side = lax.axis_index("gz"), lax.axis_index("gy")
    has = {-1: {"gz": me > 0, "gy": side > 0}, 1: {"gz": me < n - 1, "gy": side < n_gy - 1}}
    moves = transfers(rows, n_gy)

    def present(dz, dy):
        flags = [has[d][axis] for d, axis in ((dz, "gz"), (dy, "gy")) if d != 0]
        return flags[0] if len(flags) == 1 else jnp.logical_and(flags[0], flags[1])

    def toward(dz, dy):
        return {"gz": me + dz, "gy": side + dy}

    barrier = pltpu.get_barrier_semaphore()
    expected = n.bit_length() - 1 + has[-1]["gz"].astype(jnp.int32) + has[1]["gz"].astype(jnp.int32)
    for dz, dy in [(dz, dy) for dz in (-1, 0, 1) for dy in (-1, 1) if n_gy > 1]:
        @pl.when(present(dz, dy))
        def _():
            pl.semaphore_signal(barrier, inc=1, device_id=toward(dz, dy), device_id_type=MESH)
        expected = expected + present(dz, dy).astype(jnp.int32)
    rounds = n.bit_length() - 1
    near = [jnp.bitwise_xor(me, 1 << level) for level in range(rounds)]
    for other in near:
        pl.semaphore_signal(barrier, inc=1, device_id={"gz": other, "gy": side}, device_id_type=MESH)
    for dz in (-1, 1):
        @pl.when(has[dz]["gz"])
        def _():
            pl.semaphore_signal(barrier, inc=1, device_id={"gz": me + dz, "gy": side}, device_id_type=MESH)

    def spread(level):
        if level > 0:
            pl.semaphore_wait(heard.at[level - 1], 1)
        if level < rounds:
            pl.semaphore_signal(
                heard.at[level], inc=1, device_id={"gz": near[level], "gy": side}, device_id_type=MESH
            )

    own = [
        pltpu.make_async_copy(source, target, local_sem.at[slot])
        for slot, (source, target) in enumerate(
            [
                (velocity, brick.at[:, pl.ds(RADIUS, depth), pl.ds(PAD, rows)]),
                (depth_hbm, depth_rows),
                (across_hbm, across),
                (color_hbm, color),
                (extinction_hbm, extinction),
                (index_hbm, index),
            ]
        )
    ]
    for copy in own:
        copy.start()
    for dz, at in ((-1, 0), (1, RADIUS + depth)):
        @pl.when(jnp.logical_not(has[dz]["gz"]))
        def _():
            brick[:, pl.ds(at, RADIUS)] = jnp.zeros((parts, RADIUS, rows + 2 * PAD, columns), brick.dtype)
    for dy, at in ((-1, 0), (1, PAD + rows)):
        @pl.when(jnp.logical_not(has[dy]["gy"]))
        def _():
            brick[:, :, pl.ds(at, PAD)] = jnp.zeros((parts, depth + 2 * RADIUS, PAD, columns), brick.dtype)
        if EDGE < PAD:
            spare = at if dy < 0 else at + EDGE
            for z_at in (0, RADIUS + depth):
                @pl.when(has[dy]["gy"])
                def _():
                    brick[:, pl.ds(z_at, RADIUS), pl.ds(spare, PAD - EDGE)] = jnp.zeros(
                        (parts, RADIUS, PAD - EDGE, columns), brick.dtype
                    )

    def halo(slot):
        dz, dy, y_from, y_to, count, _ = moves[slot]
        z_from = {-1: pl.ds(0, RADIUS), 0: pl.ds(0, depth), 1: pl.ds(depth - RADIUS, RADIUS)}[dz]
        z_to = {-1: pl.ds(RADIUS + depth, RADIUS), 0: pl.ds(RADIUS, depth), 1: pl.ds(0, RADIUS)}[dz]
        return pltpu.make_async_remote_copy(
            src_ref=velocity.at[:, z_from, pl.ds(y_from, count)],
            dst_ref=brick.at[:, z_to, pl.ds(y_to, count)],
            send_sem=halo_send.at[slot],
            recv_sem=halo_got.at[slot],
            device_id=toward(dz, dy),
            device_id_type=MESH,
        )

    queue = [(dz, block) for dz in (1, -1) for block in range(rows // BLOCK)]

    def each(dz, block, act):
        for slot, (slot_dz, slot_dy, _, _, _, needed) in enumerate(moves):
            if slot_dz == dz and block in (None, needed):
                @pl.when(present(slot_dz, slot_dy))
                def _():
                    act(halo(slot))

    def advance(step):
        each(*queue[step], lambda copy: copy.wait_send())
        if step + IN_FLIGHT < len(queue):
            each(*queue[step + IN_FLIGHT], lambda copy: copy.start())

    pl.semaphore_wait(barrier, expected)
    for entry in queue[:IN_FLIGHT]:
        each(*entry, lambda copy: copy.start())
    each(0, None, lambda copy: copy.start())
    spread(0)

    for copy in own:
        copy.wait()
    for channel in range(4):
        before = None
        for point in range(TF_POINTS):
            entry = index[point]
            value = color[channel, entry] if channel < 3 else extinction[entry]
            table[channel * TF_POINTS + point] = jnp.full((8, columns), value if point == 0 else value - before, jnp.float32)
            before = value

    def arrived(dz, block):
        for slot, (slot_dz, slot_dy, _, _, _, needed) in enumerate(moves):
            if needed == block and (slot_dz == dz or (slot_dz == 0 and dz == 1)):
                @pl.when(present(-slot_dz, -slot_dy))
                def _():
                    halo(slot).wait_recv()

    def piece(target):
        return pltpu.make_async_remote_copy(
            src_ref=sent.at[target],
            dst_ref=got.at[me],
            send_sem=piece_send.at[target],
            recv_sem=piece_got.at[me],
            device_id={"gz": target, "gy": side},
            device_id_type=MESH,
        )

    def filtered(values, band):
        high = values.astype(jnp.bfloat16)
        low = (values - high.astype(jnp.float32)).astype(jnp.bfloat16)
        both = jnp.dot(jnp.concatenate([high, low], 1), band, preferred_element_type=jnp.float32)
        return both[:, :columns] + both[:, columns:]

    span = half * BLOCK

    def march(block, first_plane, accum, transmit):
        window = jnp.concatenate(
            [
                brick[
                    c, pl.ds(first_plane, half + 2 * RADIUS), pl.ds(block * BLOCK, BLOCK + 2 * PAD), :
                ].reshape(-1, columns)
                for c in range(parts)
            ],
            1,
        )
        both = jnp.dot(depth_rows[...], window, preferred_element_type=jnp.float32)
        smooth = both[: 3 * span] + both[3 * span :]
        grads = []
        for c in range(parts):
            lanes = slice(c * columns, (c + 1) * columns)
            along_x = filtered(smooth[:span, lanes], across[0])
            others = filtered(smooth[span:, lanes], across[1])
            grads.append([along_x, others[:span], others[span:]])
        total = grads[0][0] * grads[0][0] + grads[1][1] * grads[1][1] + grads[2][2] * grads[2][2]
        cross = grads[0][1] * grads[1][0] + grads[0][2] * grads[2][0] + grads[1][2] * grads[2][1]
        vortex = -0.5 * total - cross
        position = (TF_POINTS - 1) * jax.nn.sigmoid(vortex_gain * vortex)
        position = position.reshape(half, BLOCK // 8, 8, columns)
        for plane in range(half):
            here = position[plane]
            looked = [jnp.broadcast_to(table[ch * TF_POINTS][None], here.shape) for ch in range(4)]
            for point in range(1, TF_POINTS):
                weight = jnp.clip(here - (point - 1), 0.0, 1.0)
                for ch in range(4):
                    looked[ch] = looked[ch] + weight * table[ch * TF_POINTS + point][None]
            passed = jnp.exp(-looked[3])
            share = transmit * (1.0 - passed)
            accum = [accum[ch] + share * looked[ch] for ch in range(3)]
            transmit = transmit * passed
        return accum, transmit

    shape = (BLOCK // 8, 8, columns)
    for block in range(rows // BLOCK):
        advance(block)
        arrived(1, block)
        if 0 < block <= rounds:
            spread(block)
        accum, transmit = march(block, 0, [jnp.zeros(shape, jnp.float32)] * 3, jnp.ones(shape, jnp.float32))
        for ch in range(3):
            front[block, ch] = accum[ch]
        front[block, 3] = transmit
    for block in range(rows // BLOCK):
        advance(rows // BLOCK + block)
        arrived(-1, block)
        accum, transmit = march(block, half, [front[block, ch] for ch in range(3)], front[block, 3])
        if block == 0:
            for level in range(rows // BLOCK, rounds + 1):
                spread(level)
        image = [part.reshape(BLOCK, columns) for part in accum + [1.0 - transmit]]
        for local in range(BLOCK // group):
            target = block * (BLOCK // group) + local
            for ch in range(4):
                staged[target, pl.ds(ch * group, group), :] = image[ch][local * group : (local + 1) * group]
            slab = staged[target].astype(jnp.bfloat16)

            @pl.when(me == target)
            def _():
                got[target] = slab

            @pl.when(me != target)
            def _():
                sent[target] = slab
                piece(target).start()

    for source in range(n):
        @pl.when(me != source)
        def _():
            pltpu.make_async_remote_copy(
                src_ref=sent.at[source],
                dst_ref=got.at[source],
                send_sem=piece_send.at[source],
                recv_sem=piece_got.at[source],
                device_id={"gz": source, "gy": side},
                device_id_type=MESH,
            ).wait_recv()
    accum = [jnp.zeros((group, columns), jnp.float32) for _ in range(3)]
    transmit = jnp.ones((group, columns), jnp.float32)
    for source in range(n):
        part = got[source].astype(jnp.float32)
        for ch in range(3):
            accum[ch] = accum[ch] + transmit * part[ch * group : (ch + 1) * group]
        transmit = transmit * (1.0 - part[3 * group :])
    for ch in range(3):
        out[ch, 0] = accum[ch]
    out[3, 0] = 1.0 - transmit

    for target in range(n):
        @pl.when(me != target)
        def _():
            piece(target).wait_send()
    each(0, None, lambda copy: copy.wait_send())


def solution(mesh):
    n, n_gy = mesh.shape["gz"], mesh.shape["gy"]

    def shards(velocity, palette_color, palette_extinction, palette_index):
        parts, depth, rows, columns = velocity.shape
        group = rows // n
        depth_rows, across = operators(depth // 2, columns)
        halos = len(transfers(rows, n_gy))
        return pl.pallas_call(
            functools.partial(kernel, n, n_gy),
            out_shape=jax.ShapeDtypeStruct((4, 1, group, columns), jnp.float32),
            in_specs=[pl.BlockSpec(memory_space=pl.ANY)] * 6,
            out_specs=pl.BlockSpec(memory_space=pltpu.VMEM),
            scratch_shapes=[
                pltpu.VMEM((parts, depth + 2 * RADIUS, rows + 2 * PAD, columns), velocity.dtype),
                pltpu.VMEM(depth_rows.shape, jnp.bfloat16),
                pltpu.VMEM(across.shape, jnp.bfloat16),
                pltpu.SMEM(palette_color.shape, jnp.float32),
                pltpu.SMEM(palette_extinction.shape, jnp.float32),
                pltpu.SMEM(palette_index.shape, jnp.int32),
                pltpu.VMEM((4 * TF_POINTS, 8, columns), jnp.float32),
                pltpu.VMEM((rows // BLOCK, 4, BLOCK // 8, 8, columns), jnp.float32),
                pltpu.VMEM((n, 4 * group, columns), jnp.float32),
                pltpu.VMEM((n, 4 * group, columns), jnp.bfloat16),
                pltpu.VMEM((n, 4 * group, columns), jnp.bfloat16),
                pltpu.SemaphoreType.DMA((6,)),
                pltpu.SemaphoreType.DMA((halos,)),
                pltpu.SemaphoreType.DMA((halos,)),
                pltpu.SemaphoreType.DMA((n,)),
                pltpu.SemaphoreType.DMA((n,)),
                pltpu.SemaphoreType.REGULAR((n.bit_length() - 1,)),
            ],
            compiler_params=pltpu.CompilerParams(collective_id=0, has_side_effects=True),
        )(velocity, jnp.asarray(depth_rows), jnp.asarray(across), palette_color, palette_extinction, palette_index)

    return jax.shard_map(
        shards,
        mesh=mesh,
        in_specs=(P(None, "gz", "gy", None), P(), P(), P()),
        out_specs=P(None, "gy", "gz", None),
        check_vma=False,
    )
```

profile of v0, /device:TPU:0, one launch (start us, length us, event | category | flops | bytes accessed | tf_op | source)
XLA Modules:
  0.0 24.2 jit_solution(1648930346592786282)
XLA Ops:
  0.0 22.9 %shard_map.64 = f32[4,1,4,128]{3,2,1,0:T(4,128)} custom-call(bf16[3,8,64,128]{3,2,1,0:T(8,128)(2,1)} %velocity.1, bf16[384,384]{1,0:T(8,128)(2,1)} %constant.4.clone.depth_hbm, bf16[2,256,256]{2,1,0:T(8,128)(2,1)} %constant.5.clone.across_hbm, f32[3,64]{1,0:T(4,128)} %color_hbm.1, f32[64]{0:T(128)} %extinction_hbm.1, s32[16]{0:T(128)} %index_hbm.1), custom_call_target="tpu_custom_call" | custom-call | tf_op jit(solution)/shard_map/pallas_call | solution.py:331
  22.9 1.3 %copy.8 = f32[4,1,4,128]{3,2,1,0:T(4,128)} copy(f32[4,1,4,128]{3,2,1,0:T(4,128)} %shard_map.64) | data formatting | bytes 16384
where the time goes:
time: 24.4 us; the launch traced here: 24.2 us
  Pallas kernels  22.9 us (94%)
  local copies, waits for them, and re-layouts  1.3 us (5%)
    pallas_call x1, Pallas kernels, shards(): pl.pallas_call(functools.partial(kernel, n, n_gy), out_shape=jax.ShapeDty...  22.9 us
    unnamed x1, local copies, waits for them, and re-layouts  1.3 us

commit v1 on v0

--- a/solution.py
+++ b/solution.py
@@ -330,7 +330,7 @@
         halos = len(transfers(rows, n_gy))
         return pl.pallas_call(
             functools.partial(kernel, n, n_gy),
-            out_shape=jax.ShapeDtypeStruct((4, 1, group, columns), jnp.float32),
+            out_shape=pltpu.VMEM((4, 1, group, columns), jnp.float32),
             in_specs=[pl.BlockSpec(memory_space=pl.ANY)] * 6,
             out_specs=pl.BlockSpec(memory_space=pltpu.VMEM),
             scratch_shapes=[

time: 24.4 us -> 23 us (0.943)
  local copies, waits for them, and re-layouts: 1.3 us -> 0.6 us
  Pallas kernels: 22.9 us -> 22.3 us
    unnamed x1, local copies, waits for them, and re-layouts: 1.3 us -> 0.6 us
    pallas_call x1, Pallas kernels: 22.9 us -> 22.3 us  [shards(): pl.pallas_call(functools.partial(kernel, n, n_gy), out_shape=pltpu.VMEM((...]
where the time goes in v1:
time: 23 us; the launch traced here: 22.9 us
  Pallas kernels  22.3 us (97%)
  local copies, waits for them, and re-layouts  0.6 us (3%)
    pallas_call x1, Pallas kernels, shards(): pl.pallas_call(functools.partial(kernel, n, n_gy), out_shape=pltpu.VMEM((...  22.3 us
    unnamed x1, local copies, waits for them, and re-layouts  0.6 us

profile of v1, /device:TPU:0, one launch (start us, length us, event | category | flops | bytes accessed | tf_op | source)
XLA Modules:
  0.0 22.9 jit_solution(11855496657848873791)
XLA Ops:
  0.0 22.3 %shard_map.64 = f32[4,1,4,128]{3,2,1,0:T(4,128)S(1)} custom-call(bf16[3,8,64,128]{3,2,1,0:T(8,128)(2,1)} %velocity.1, bf16[384,384]{1,0:T(8,128)(2,1)} %constant.4.clone.depth_hbm, bf16[2,256,256]{2,1,0:T(8,128)(2,1)} %constant.5.clone.across_hbm, f32[3,64]{1,0:T(4,128)} %color_hbm.1, f32[64]{0:T(128)} %extinction_hbm.1, s32[16]{0:T(128)} %index_hbm.1), custom_call_target="tpu_custom_call" | custom-call | tf_op jit(solution)/shard_map/pallas_call | solution.py:331
  22.3 0.6 %copy.8 = f32[4,1,4,128]{3,2,1,0:T(4,128)} copy(f32[4,1,4,128]{3,2,1,0:T(4,128)S(1)} %shard_map.64) | data formatting | bytes 16384

commit v2 on v1

v2 whole, which is shorter than its diff:
```python
import functools
import math

import jax
import jax.numpy as jnp
import numpy as np
from jax import lax
from jax.experimental import pallas as pl
from jax.experimental.pallas import tpu as pltpu
from jax.sharding import PartitionSpec as P

RADIUS = 4
TF_POINTS = 16
SUB = 8
BLOCK = 16
PLANE = 4
IN_FLIGHT = 3
MESH = pl.DeviceIdType.MESH
FAR, NEAR, LEVEL = 0, 1, 2

filter_sigma = 1.5
vortex_gain = 400.0


def filter_taps():
    weights = [
        math.exp(-((offset - RADIUS) ** 2) / (2.0 * filter_sigma**2))
        for offset in range(2 * RADIUS + 1)
    ]
    weight_sum = sum(weights)
    gauss = [weight / weight_sum for weight in weights]
    moment = sum(((offset - RADIUS) ** 2 * gauss[offset] for offset in range(2 * RADIUS + 1)))
    deriv = [(offset - RADIUS) * gauss[offset] / moment for offset in range(2 * RADIUS + 1)]
    return (gauss, deriv)


def banded(taps, outs, ins, shift):
    band = np.zeros((outs, ins), np.float64)
    for i in range(outs):
        for offset in range(2 * RADIUS + 1):
            k = i + shift + offset - RADIUS
            if 0 <= k < ins:
                band[i, k] = taps[offset]
    return band


def high_low(band):
    band = band.astype(np.float32)
    high = band.astype(jnp.bfloat16)
    low = (band - high.astype(np.float32)).astype(jnp.bfloat16)
    return high, low


def operators(half, columns):
    gauss, deriv = filter_taps()
    z_of = [banded(taps, half, half + 2 * RADIUS, RADIUS) for taps in (gauss, deriv)]
    y_of = [banded(taps, SUB, SUB + 2 * RADIUS, RADIUS) for taps in (gauss, deriv)]
    both = np.concatenate([np.kron(z_of[0], y_of[0]), np.kron(z_of[0], y_of[1]), np.kron(z_of[1], y_of[0])], 0)
    depth_rows = np.concatenate(high_low(both), 0)
    across = []
    for taps in (deriv, gauss):
        high, low = high_low(banded(taps, columns, columns, 0).T)
        across.append(np.block([[high, low], [high, np.zeros_like(low)]]))
    return depth_rows, np.stack(across)


def steps(rows):
    blocks = rows // BLOCK
    order = [(kind, block) for block in range(blocks) for kind in (FAR, NEAR)]
    if blocks > 1:
        order[-4:] = [(FAR, blocks - 2), (FAR, blocks - 1), (NEAR, blocks - 2), (NEAR, blocks - 1)]
    return order


def transfers(rows, n_gy):
    blocks = rows // BLOCK
    ends = [min(rows, (block + 1) * BLOCK + SUB) for block in range(blocks)]
    edges = [(1, rows - RADIUS, 0, RADIUS, 0), (-1, 0, RADIUS + rows, RADIUS, blocks - 1)] if n_gy > 1 else []
    moves = [(LEVEL, *edge) for edge in edges]
    for kind in (FAR, NEAR):
        start = 0
        for block, end in enumerate(ends):
            moves += [(kind, *edge) for edge in edges if edge[-1] == block]
            if end > start:
                moves.append((kind, 0, start, RADIUS + start, end - start, block))
            start = end
    return moves


def kernel(
    n, n_gy, velocity, depth_hbm, across_hbm, color_hbm, extinction_hbm, index_hbm, out,
    brick, depth_rows, across, color, extinction, index, table, staged, sent, got,
    local_sem, halo_send, halo_got, piece_send, piece_got, heard,
):
    parts, depth, rows, columns = velocity.shape
    half = depth // 2
    group = rows // n
    layers = n // PLANE
    me, side = lax.axis_index("gz"), lax.axis_index("gy")
    odd = lax.rem(me, 2)
    layer = me // PLANE
    near, far = me + 1 - 2 * odd, me - 1 + 2 * odd
    has_far = jnp.logical_and(far >= 0, far < n)
    has_row = {-1: side > 0, 1: side < n_gy - 1}
    has_layer = {-1: layer > 0, 1: layer < layers - 1}
    moves = transfers(rows, n_gy)
    order = steps(rows)
    row_ways = (-1, 1) if n_gy > 1 else ()

    def present(kind, dy):
        flags = ([has_far] if kind == FAR else []) + ([has_row[dy]] if dy else [])
        if not flags:
            return None
        return flags[0] if len(flags) == 1 else jnp.logical_and(flags[0], flags[1])

    def only(flag, act):
        if flag is None:
            act()
        else:
            pl.when(flag)(act)

    def toward(kind, dy):
        return {"gz": {FAR: far, NEAR: near, LEVEL: me}[kind], "gy": side + dy}

    own = [
        pltpu.make_async_copy(source, target, local_sem.at[slot])
        for slot, (source, target) in enumerate(
            [
                (velocity, brick.at[:, pl.ds(RADIUS, depth), pl.ds(RADIUS, rows)]),
                (depth_hbm, depth_rows),
                (across_hbm, across),
                (color_hbm, color),
                (extinction_hbm, extinction),
                (index_hbm, index),
            ]
        )
    ]

    barrier = pltpu.get_barrier_semaphore()
    expected = jnp.int32(0)
    greeted = [(toward(kind, dy), present(kind, dy)) for kind in (FAR, NEAR, LEVEL) for dy in (0, *row_ways) if kind != LEVEL or dy]
    greeted.append(({"gz": jnp.bitwise_xor(me, 2), "gy": side}, None))
    greeted += [({"gz": me + PLANE * way, "gy": side}, has_layer[way]) for way in (-1, 1)]
    for target, flag in greeted:
        def greet(target=target):
            pl.semaphore_signal(barrier, inc=1, device_id=target, device_id_type=MESH)
        only(flag, greet)
        expected = expected + (1 if flag is None else flag.astype(jnp.int32))

    for copy in own:
        copy.start()

    @pl.when(jnp.logical_not(has_far))
    def _():
        brick[:, pl.ds(odd * (RADIUS + depth), RADIUS)] = jnp.zeros((parts, RADIUS, rows + 2 * RADIUS, columns), brick.dtype)
    for dy, at in ((-1, 0), (1, RADIUS + rows)):
        @pl.when(jnp.logical_not(has_row[dy]))
        def _():
            brick[:, :, pl.ds(at, RADIUS)] = jnp.zeros((parts, depth + 2 * RADIUS, RADIUS, columns), brick.dtype)

    def halo(slot):
        kind, dy, y_from, y_to, count, _ = moves[slot]
        up = {FAR: odd, NEAR: 1 - odd, LEVEL: None}[kind]
        if kind == LEVEL:
            z_from, z_to = pl.ds(0, depth), pl.ds(RADIUS, depth)
        else:
            z_from, z_to = pl.ds(up * (depth - RADIUS), RADIUS), pl.ds((1 - up) * (RADIUS + depth), RADIUS)
        return pltpu.make_async_remote_copy(
            src_ref=velocity.at[:, z_from, pl.ds(y_from, count)],
            dst_ref=brick.at[:, z_to, pl.ds(y_to, count)],
            send_sem=halo_send.at[slot],
            recv_sem=halo_got.at[slot],
            device_id=toward(kind, dy),
            device_id_type=MESH,
        )

    def each(kind, block, act):
        for slot, (slot_kind, slot_dy, _, _, _, needed) in enumerate(moves):
            if slot_kind == kind and block in (None, needed):
                only(present(slot_kind, slot_dy), functools.partial(act, slot))

    def launch(slot):
        halo(slot).start()

    def advance(step):
        each(*order[step], lambda slot: halo(slot).wait_send())
        if step + IN_FLIGHT < len(order):
            each(*order[step + IN_FLIGHT], launch)

    def arrived(kind, block, level):
        for slot, (slot_kind, slot_dy, _, _, _, needed) in enumerate(moves):
            if needed == block and (slot_kind == kind or (slot_kind == LEVEL and level)):
                def take(slot=slot):
                    halo(slot).wait_recv()
                only(present(slot_kind, -slot_dy), take)

    pl.semaphore_wait(barrier, expected)
    for entry in order[:IN_FLIGHT]:
        each(*entry, launch)
    each(LEVEL, None, launch)

    def tell(slot, target):
        pl.semaphore_signal(heard.at[slot], inc=1, device_id={"gz": target, "gy": side}, device_id_type=MESH)

    def token(slot, came, target, goes):
        @pl.when(came)
        def _():
            pl.semaphore_wait(heard.at[slot], 1)

        @pl.when(goes)
        def _():
            tell(slot, target)

    tell(0, jnp.bitwise_xor(me, 1))
    pl.semaphore_wait(heard.at[0], 1)
    tell(1, jnp.bitwise_xor(me, 2))
    for copy in own[3:]:
        copy.wait()
    lane = lax.broadcasted_iota(jnp.int32, (SUB, columns), 1)
    for channel in range(4):
        values = []
        for point in range(TF_POINTS):
            entry = index[point]
            values.append(color[channel, entry] if channel < 3 else extinction[entry])
        level = jnp.zeros((SUB, columns), jnp.float32)
        slope = jnp.zeros((SUB, columns), jnp.float32)
        for point in range(TF_POINTS):
            level = jnp.where(lane == point, values[point], level)
            if point + 1 < TF_POINTS:
                slope = jnp.where(lane == point, values[point + 1] - values[point], slope)
        table[2 * channel] = level
        table[2 * channel + 1] = slope
    pl.semaphore_wait(heard.at[1], 1)
    token(2, has_layer[-1], me + PLANE, has_layer[1])
    token(3, has_layer[1], me - PLANE, has_layer[-1])
    for copy in own[:3]:
        copy.wait()

    def piece(target):
        return pltpu.make_async_remote_copy(
            src_ref=sent.at[target],
            dst_ref=got.at[me],
            send_sem=piece_send.at[target],
            recv_sem=piece_got.at[me],
            device_id={"gz": target, "gy": side},
            device_id_type=MESH,
        )

    def filtered(values, band):
        high = values.astype(jnp.bfloat16)
        low = (values - high.astype(jnp.float32)).astype(jnp.bfloat16)
        both = jnp.dot(jnp.concatenate([high, low], 1), band, preferred_element_type=jnp.float32)
        return both[:, :columns] + both[:, columns:]

    subs = BLOCK // SUB
    span = half * SUB

    def march(kind, block):
        upper = {FAR: odd, NEAR: 1 - odd}[kind]
        window = jnp.concatenate(
            [
                brick[
                    c, pl.ds(upper * half, half + 2 * RADIUS), pl.ds(block * BLOCK + sub * SUB, SUB + 2 * RADIUS), :
                ].reshape(-1, columns)
                for sub in range(subs)
                for c in range(parts)
            ],
            1,
        )
        both = jnp.dot(depth_rows[...], window, preferred_element_type=jnp.float32)
        smooth = both[: 3 * span] + both[3 * span :]
        cut = [smooth[:, at * columns : (at + 1) * columns] for at in range(subs * parts)]
        along_x = filtered(jnp.concatenate([one[:span] for one in cut], 0), across[0])
        others = filtered(jnp.concatenate([one[span:] for one in cut], 0), across[1])
        halves = []
        for sub in range(subs):
            grads = []
            for c in range(parts):
                at = sub * parts + c
                grads.append([
                    along_x[at * span : (at + 1) * span],
                    others[2 * at * span : (2 * at + 1) * span],
                    others[(2 * at + 1) * span : (2 * at + 2) * span],
                ])
            total = grads[0][0] * grads[0][0] + grads[1][1] * grads[1][1] + grads[2][2] * grads[2][2]
            cross = grads[0][1] * grads[1][0] + grads[0][2] * grads[2][0] + grads[1][2] * grads[2][1]
            vortex = -0.5 * total - cross
            position = (TF_POINTS - 1) * jax.nn.sigmoid(vortex_gain * vortex)
            accum, transmit = None, None
            for plane in range(half):
                here = position[plane * SUB : (plane + 1) * SUB]
                point = here.astype(jnp.int32)
                past = here - point.astype(jnp.float32)
                looked = [
                    jnp.take_along_axis(table[2 * ch], point, axis=1, mode="promise_in_bounds")
                    + past * jnp.take_along_axis(table[2 * ch + 1], point, axis=1, mode="promise_in_bounds")
                    for ch in range(4)
                ]
                passed = jnp.exp(-looked[3])
                if plane == 0:
                    share = 1.0 - passed
                    accum, transmit = [share * looked[ch] for ch in range(3)], passed
                else:
                    share = transmit * (1.0 - passed)
                    accum = [accum[ch] + share * looked[ch] for ch in range(3)]
                    transmit = transmit * passed
            halves.append(accum + [transmit])
        return [jnp.concatenate([part[ch] for part in halves], 0) for ch in range(4)]

    done = {}
    for step, (kind, block) in enumerate(order):
        advance(step)
        arrived(kind, block, (NEAR, block) not in done and (FAR, block) not in done)
        done[kind, block] = march(kind, block)
        if (1 - kind, block) not in done:
            continue
        first = [jnp.where(odd == 0, done[FAR, block][ch], done[NEAR, block][ch]) for ch in range(4)]
        then = [jnp.where(odd == 0, done[NEAR, block][ch], done[FAR, block][ch]) for ch in range(4)]
        image = [first[ch] + first[3] * then[ch] for ch in range(3)] + [1.0 - first[3] * then[3]]
        for local in range(BLOCK // group):
            target = block * (BLOCK // group) + local
            for ch in range(4):
                staged[target, pl.ds(ch * group, group), :] = image[ch][local * group : (local + 1) * group]
            slab = staged[target].astype(jnp.bfloat16)

            @pl.when(me == target)
            def _():
                got[target] = slab

            @pl.when(me != target)
            def _():
                sent[target] = slab
                piece(target).start()

    accum = [jnp.zeros((group, columns), jnp.float32) for _ in range(3)]
    transmit = jnp.ones((group, columns), jnp.float32)
    for source in range(n):
        @pl.when(me != source)
        def _():
            pltpu.make_async_remote_copy(
                src_ref=sent.at[source],
                dst_ref=got.at[source],
                send_sem=piece_send.at[source],
                recv_sem=piece_got.at[source],
                device_id={"gz": source, "gy": side},
                device_id_type=MESH,
            ).wait_recv()
    for source in range(n):
        part = got[source].astype(jnp.float32)
        for ch in range(3):
            accum[ch] = accum[ch] + transmit * part[ch * group : (ch + 1) * group]
        transmit = transmit * (1.0 - part[3 * group :])
    for ch in range(3):
        out[ch, 0] = accum[ch]
    out[3, 0] = 1.0 - transmit

    for target in range(n):
        @pl.when(me != target)
        def _():
            piece(target).wait_send()
    each(LEVEL, None, lambda slot: halo(slot).wait_send())


def solution(mesh):
    n, n_gy = mesh.shape["gz"], mesh.shape["gy"]

    def shards(velocity, palette_color, palette_extinction, palette_index):
        parts, depth, rows, columns = velocity.shape
        group = rows // n
        depth_rows, across = operators(depth // 2, columns)
        halos = len(transfers(rows, n_gy))
        return pl.pallas_call(
            functools.partial(kernel, n, n_gy),
            out_shape=pltpu.VMEM((4, 1, group, columns), jnp.float32),
            in_specs=[pl.BlockSpec(memory_space=pl.ANY)] * 6,
            out_specs=pl.BlockSpec(memory_space=pltpu.VMEM),
            scratch_shapes=[
                pltpu.VMEM((parts, depth + 2 * RADIUS, rows + 2 * RADIUS, columns), velocity.dtype),
                pltpu.VMEM(depth_rows.shape, jnp.bfloat16),
                pltpu.VMEM(across.shape, jnp.bfloat16),
                pltpu.SMEM(palette_color.shape, jnp.float32),
                pltpu.SMEM(palette_extinction.shape, jnp.float32),
                pltpu.SMEM(palette_index.shape, jnp.int32),
                pltpu.VMEM((8, SUB, columns), jnp.float32),
                pltpu.VMEM((n, 4 * group, columns), jnp.float32),
                pltpu.VMEM((n, 4 * group, columns), jnp.bfloat16),
                pltpu.VMEM((n, 4 * group, columns), jnp.bfloat16),
                pltpu.SemaphoreType.DMA((6,)),
                pltpu.SemaphoreType.DMA((halos,)),
                pltpu.SemaphoreType.DMA((halos,)),
                pltpu.SemaphoreType.DMA((n,)),
                pltpu.SemaphoreType.DMA((n,)),
                pltpu.SemaphoreType.REGULAR((4,)),
            ],
            compiler_params=pltpu.CompilerParams(collective_id=0, has_side_effects=True),
        )(velocity, jnp.asarray(depth_rows), jnp.asarray(across), palette_color, palette_extinction, palette_index)

    return jax.shard_map(
        shards,
        mesh=mesh,
        in_specs=(P(None, "gz", "gy", None), P(), P(), P()),
        out_specs=P(None, "gy", "gz", None),
        check_vma=False,
    )
```

time: 23 us -> 23.7 us (1.030)
  Pallas kernels: 22.3 us -> 23 us
    pallas_call x1, Pallas kernels: 22.3 us -> 23 us  [shards(): pl.pallas_call(functools.partial(kernel, n, n_gy), out_shape=pltpu.VMEM((...]
where the time goes in v2:
time: 23.7 us; the launch traced here: 23.6 us
  Pallas kernels  23 us (97%)
  local copies, waits for them, and re-layouts  0.6 us (3%)
    pallas_call x1, Pallas kernels, shards(): pl.pallas_call(functools.partial(kernel, n, n_gy), out_shape=pltpu.VMEM((...  23 us
    unnamed x1, local copies, waits for them, and re-layouts  0.6 us

profile of v2, /device:TPU:0, one launch (start us, length us, event | category | flops | bytes accessed | tf_op | source)
XLA Modules:
  0.0 23.6 jit_solution(3901883643006113778)
XLA Ops:
  0.0 23.0 %shard_map.64 = f32[4,1,4,128]{3,2,1,0:T(4,128)S(1)} custom-call(bf16[3,8,64,128]{3,2,1,0:T(8,128)(2,1)} %velocity.1, bf16[192,192]{1,0:T(8,128)(2,1)} %constant.4.clone.depth_hbm, bf16[2,256,256]{2,1,0:T(8,128)(2,1)} %constant.5.clone.across_hbm, f32[3,64]{1,0:T(4,128)} %color_hbm.1, f32[64]{0:T(128)} %extinction_hbm.1, s32[16]{0:T(128)} %index_hbm.1), custom_call_target="tpu_custom_call" | custom-call | tf_op jit(solution)/shard_map/pallas_call | solution.py:372
  23.0 0.6 %copy.8 = f32[4,1,4,128]{3,2,1,0:T(4,128)} copy(f32[4,1,4,128]{3,2,1,0:T(4,128)S(1)} %shard_map.64) | data formatting | bytes 16384

commit v3 on v2

--- a/solution.py
+++ b/solution.py
@@ -14,7 +14,6 @@
 SUB = 8
 BLOCK = 16
 PLANE = 4
-IN_FLIGHT = 3
 MESH = pl.DeviceIdType.MESH
 FAR, NEAR, LEVEL = 0, 1, 2
 
@@ -182,11 +181,6 @@
     def launch(slot):
         halo(slot).start()
 
-    def advance(step):
-        each(*order[step], lambda slot: halo(slot).wait_send())
-        if step + IN_FLIGHT < len(order):
-            each(*order[step + IN_FLIGHT], launch)
-
     def arrived(kind, block, level):
         for slot, (slot_kind, slot_dy, _, _, _, needed) in enumerate(moves):
             if needed == block and (slot_kind == kind or (slot_kind == LEVEL and level)):
@@ -195,25 +189,57 @@
                 only(present(slot_kind, -slot_dy), take)
 
     pl.semaphore_wait(barrier, expected)
-    for entry in order[:IN_FLIGHT]:
-        each(*entry, launch)
+    first = me == 1
+
+    @pl.when(first)
+    def _():
+        for kind, block in order:
+            each(1 - kind, block, launch)
+
+    @pl.when(jnp.logical_not(first))
+    def _():
+        for kind, block in order:
+            each(kind, block, launch)
+
     each(LEVEL, None, launch)
 
     def tell(slot, target):
         pl.semaphore_signal(heard.at[slot], inc=1, device_id={"gz": target, "gy": side}, device_id_type=MESH)
 
-    def token(slot, came, target, goes):
-        @pl.when(came)
+    blocks = rows // BLOCK
+    last_layer = [((block + 1) * BLOCK // group - 1) // PLANE for block in range(blocks)]
+    done_at = [max(order.index((FAR, block)), order.index((NEAR, block))) for block in range(blocks)]
+
+    @pl.when(has_layer[1])
+    def _():
+        pl.when(has_layer[-1])(lambda: pl.semaphore_wait(heard.at[0], 1))
+        tell(0, me + PLANE)
+
+    def down(distance):
+        @pl.when(layer + distance < layers)
         def _():
-            pl.semaphore_wait(heard.at[slot], 1)
-
-        @pl.when(goes)
-        def _():
-            tell(slot, target)
-
-    tell(0, jnp.bitwise_xor(me, 1))
-    pl.semaphore_wait(heard.at[0], 1)
-    tell(1, jnp.bitwise_xor(me, 2))
+            pl.semaphore_wait(heard.at[distance], 1)
+
+        if distance + 1 < layers:
+            @pl.when(jnp.logical_and(layer + distance < layers, has_layer[-1]))
+            def _():
+                tell(distance + 1, me - PLANE)
+
+    reached = [-1, 0]
+
+    def learn(step):
+        goal = max([(step + 2) // 2] + [last_layer[block] for block in range(blocks) if done_at[block] <= step + 1])
+        for distance in range(reached[1] + 1, min(goal, layers - 1) + 1):
+            down(distance)
+            reached[1] = distance
+        for block in range(reached[0] + 1, blocks):
+            if last_layer[block] <= reached[1]:
+                tell(layers + block, near)
+                reached[0] = block
+
+    @pl.when(has_layer[-1])
+    def _():
+        tell(1, me - PLANE)
     for copy in own[3:]:
         copy.wait()
     lane = lax.broadcasted_iota(jnp.int32, (SUB, columns), 1)
@@ -230,11 +256,12 @@
                 slope = jnp.where(lane == point, values[point + 1] - values[point], slope)
         table[2 * channel] = level
         table[2 * channel + 1] = slope
-    pl.semaphore_wait(heard.at[1], 1)
-    token(2, has_layer[-1], me + PLANE, has_layer[1])
-    token(3, has_layer[1], me - PLANE, has_layer[-1])
     for copy in own[:3]:
         copy.wait()
+
+    @pl.when(jnp.logical_and(has_layer[-1], jnp.logical_not(has_layer[1])))
+    def _():
+        pl.semaphore_wait(heard.at[0], 1)
 
     def piece(target):
         return pltpu.make_async_remote_copy(
@@ -309,14 +336,15 @@
 
     done = {}
     for step, (kind, block) in enumerate(order):
-        advance(step)
         arrived(kind, block, (NEAR, block) not in done and (FAR, block) not in done)
         done[kind, block] = march(kind, block)
+        learn(step)
         if (1 - kind, block) not in done:
             continue
-        first = [jnp.where(odd == 0, done[FAR, block][ch], done[NEAR, block][ch]) for ch in range(4)]
-        then = [jnp.where(odd == 0, done[NEAR, block][ch], done[FAR, block][ch]) for ch in range(4)]
-        image = [first[ch] + first[3] * then[ch] for ch in range(3)] + [1.0 - first[3] * then[3]]
+        pl.semaphore_wait(heard.at[layers + block], 1)
+        front = [jnp.where(odd == 0, done[FAR, block][ch], done[NEAR, block][ch]) for ch in range(4)]
+        back = [jnp.where(odd == 0, done[NEAR, block][ch], done[FAR, block][ch]) for ch in range(4)]
+        image = [front[ch] + front[3] * back[ch] for ch in range(3)] + [1.0 - front[3] * back[3]]
         for local in range(BLOCK // group):
             target = block * (BLOCK // group) + local
             for ch in range(4):
@@ -358,7 +386,8 @@
         @pl.when(me != target)
         def _():
             piece(target).wait_send()
-    each(LEVEL, None, lambda slot: halo(slot).wait_send())
+    for kind in (FAR, NEAR, LEVEL):
+        each(kind, None, lambda slot: halo(slot).wait_send())
 
 
 def solution(mesh):
@@ -390,7 +419,7 @@
                 pltpu.SemaphoreType.DMA((halos,)),
                 pltpu.SemaphoreType.DMA((n,)),
                 pltpu.SemaphoreType.DMA((n,)),
-                pltpu.SemaphoreType.REGULAR((4,)),
+                pltpu.SemaphoreType.REGULAR((n // PLANE + rows // BLOCK,)),
             ],
             compiler_params=pltpu.CompilerParams(collective_id=0, has_side_effects=True),
         )(velocity, jnp.asarray(depth_rows), jnp.asarray(across), palette_color, palette_extinction, palette_index)

time: 23.7 us -> 20 us (0.84)
  Pallas kernels: 23 us -> 19 us
    pallas_call x1, Pallas kernels: 23 us -> 19 us  [shards(): pl.pallas_call(functools.partial(kernel, n, n_gy), out_shape=pltpu.VMEM((...]
where the time goes in v3:
time: 20 us; the launch traced here: 19.6 us
  Pallas kernels  19 us (95%)
  local copies, waits for them, and re-layouts  0.6 us (3%)
    pallas_call x1, Pallas kernels, shards(): pl.pallas_call(functools.partial(kernel, n, n_gy), out_shape=pltpu.VMEM((...  19 us
    unnamed x1, local copies, waits for them, and re-layouts  0.6 us

profile of v3, /device:TPU:0, one launch (start us, length us, event | category | flops | bytes accessed | tf_op | source)
XLA Modules:
  0.0 19.6 jit_solution(498255699467954483)
XLA Ops:
  0.0 19.0 %shard_map.64 = f32[4,1,4,128]{3,2,1,0:T(4,128)S(1)} custom-call(bf16[3,8,64,128]{3,2,1,0:T(8,128)(2,1)} %velocity.1, bf16[192,192]{1,0:T(8,128)(2,1)} %constant.4.clone.depth_hbm, bf16[2,256,256]{2,1,0:T(8,128)(2,1)} %constant.5.clone.across_hbm, f32[3,64]{1,0:T(4,128)} %color_hbm.1, f32[64]{0:T(128)} %extinction_hbm.1, s32[16]{0:T(128)} %index_hbm.1), custom_call_target="tpu_custom_call" | custom-call | tf_op jit(solution)/shard_map/pallas_call | solution.py:401
  19.0 0.6 %copy.8 = f32[4,1,4,128]{3,2,1,0:T(4,128)} copy(f32[4,1,4,128]{3,2,1,0:T(4,128)S(1)} %shard_map.64) | data formatting | bytes 16384

commit v4 on v3

--- a/solution.py
+++ b/solution.py
@@ -16,6 +16,7 @@
 PLANE = 4
 MESH = pl.DeviceIdType.MESH
 FAR, NEAR, LEVEL = 0, 1, 2
+EARLY = -1
 
 filter_sigma = 1.5
 vortex_gain = 400.0
@@ -73,16 +74,18 @@
 
 def transfers(rows, n_gy):
     blocks = rows // BLOCK
-    ends = [min(rows, (block + 1) * BLOCK + SUB) for block in range(blocks)]
-    edges = [(1, rows - RADIUS, 0, RADIUS, 0), (-1, 0, RADIUS + rows, RADIUS, blocks - 1)] if n_gy > 1 else []
-    moves = [(LEVEL, *edge) for edge in edges]
+    top = rows - RADIUS if n_gy > 1 else rows
+    ends = [min(top, (block + 1) * BLOCK + SUB) for block in range(blocks)]
+    moves = []
     for kind in (FAR, NEAR):
         start = 0
         for block, end in enumerate(ends):
-            moves += [(kind, *edge) for edge in edges if edge[-1] == block]
             if end > start:
                 moves.append((kind, 0, start, RADIUS + start, end - start, block))
             start = end
+    if n_gy > 1:
+        moves += [(kind, 0, top, RADIUS + top, RADIUS, EARLY) for kind in (FAR, NEAR)]
+        moves += [(kind, *edge) for kind in (LEVEL, FAR, NEAR) for edge in ((1, top, 0, RADIUS, 0), (-1, 0, RADIUS + rows, RADIUS, blocks - 1))]
     return moves
 
 
@@ -137,7 +140,7 @@
 
     barrier = pltpu.get_barrier_semaphore()
     expected = jnp.int32(0)
-    greeted = [(toward(kind, dy), present(kind, dy)) for kind in (FAR, NEAR, LEVEL) for dy in (0, *row_ways) if kind != LEVEL or dy]
+    greeted = [(toward(kind, dy), present(kind, dy)) for kind, dy in [(FAR, 0), (NEAR, 0), *((LEVEL, way) for way in row_ways)]]
     greeted.append(({"gz": jnp.bitwise_xor(me, 2), "gy": side}, None))
     greeted += [({"gz": me + PLANE * way, "gy": side}, has_layer[way]) for way in (-1, 1)]
     for target, flag in greeted:
@@ -160,36 +163,50 @@
     def halo(slot):
         kind, dy, y_from, y_to, count, _ = moves[slot]
         up = {FAR: odd, NEAR: 1 - odd, LEVEL: None}[kind]
-        if kind == LEVEL:
+        source, row_from = velocity, y_from
+        if kind != LEVEL and dy:
+            z_from = z_to = pl.ds({FAR: odd, NEAR: 1 - odd}[kind] * (RADIUS + depth), RADIUS)
+            source, row_from = brick, RADIUS + y_from
+        elif kind == LEVEL:
             z_from, z_to = pl.ds(0, depth), pl.ds(RADIUS, depth)
         else:
             z_from, z_to = pl.ds(up * (depth - RADIUS), RADIUS), pl.ds((1 - up) * (RADIUS + depth), RADIUS)
         return pltpu.make_async_remote_copy(
-            src_ref=velocity.at[:, z_from, pl.ds(y_from, count)],
+            src_ref=source.at[:, z_from, pl.ds(row_from, count)],
             dst_ref=brick.at[:, z_to, pl.ds(y_to, count)],
             send_sem=halo_send.at[slot],
             recv_sem=halo_got.at[slot],
-            device_id=toward(kind, dy),
+            device_id=toward(LEVEL if dy else kind, dy),
             device_id_type=MESH,
         )
 
     def each(kind, block, act):
         for slot, (slot_kind, slot_dy, _, _, _, needed) in enumerate(moves):
-            if slot_kind == kind and block in (None, needed):
+            if slot_kind == kind and block in (None, needed) and (block is None or kind == LEVEL or slot_dy == 0):
                 only(present(slot_kind, slot_dy), functools.partial(act, slot))
 
     def launch(slot):
         halo(slot).start()
 
     def arrived(kind, block, level):
-        for slot, (slot_kind, slot_dy, _, _, _, needed) in enumerate(moves):
+        for slot, (slot_kind, slot_dy, _, _, _, needed) in sorted(enumerate(moves), key=lambda move: abs(move[1][1])):
             if needed == block and (slot_kind == kind or (slot_kind == LEVEL and level)):
                 def take(slot=slot):
                     halo(slot).wait_recv()
                 only(present(slot_kind, -slot_dy), take)
 
     pl.semaphore_wait(barrier, expected)
+    def take(kind):
+        each(kind, EARLY, lambda slot: halo(slot).wait_recv())
+
+    def relay(kind, way):
+        for slot, (slot_kind, slot_dy, *_) in enumerate(moves):
+            if slot_kind == kind and slot_dy == way:
+                only(present(kind, way), functools.partial(launch, slot))
+
     first = me == 1
+    for kind in (FAR, NEAR):
+        each(kind, EARLY, launch)
 
     @pl.when(first)
     def _():
@@ -336,7 +353,12 @@
 
     done = {}
     for step, (kind, block) in enumerate(order):
+        if block == 0 and row_ways:
+            take(kind)
+            relay(kind, 1)
         arrived(kind, block, (NEAR, block) not in done and (FAR, block) not in done)
+        if block == 0 and row_ways:
+            relay(kind, -1)
         done[kind, block] = march(kind, block)
         learn(step)
         if (1 - kind, block) not in done:

time: 20 us -> 19.6 us (0.980)
  Pallas kernels: 19 us -> 18.7 us
    pallas_call x1, Pallas kernels: 19 us -> 18.7 us  [shards(): pl.pallas_call(functools.partial(kernel, n, n_gy), out_shape=pltpu.VMEM((...]
where the time goes in v4:
time: 19.6 us; the launch traced here: 19.3 us
  Pallas kernels  18.7 us (95%)
  local copies, waits for them, and re-layouts  0.6 us (3%)
    pallas_call x1, Pallas kernels, shards(): pl.pallas_call(functools.partial(kernel, n, n_gy), out_shape=pltpu.VMEM((...  18.7 us
    unnamed x1, local copies, waits for them, and re-layouts  0.6 us

profile of v4, /device:TPU:0, one launch (start us, length us, event | category | flops | bytes accessed | tf_op | source)
XLA Modules:
  0.0 19.3 jit_solution(5031016539798998939)
XLA Ops:
  0.0 18.7 %shard_map.64 = f32[4,1,4,128]{3,2,1,0:T(4,128)S(1)} custom-call(bf16[3,8,64,128]{3,2,1,0:T(8,128)(2,1)} %velocity.1, bf16[192,192]{1,0:T(8,128)(2,1)} %constant.4.clone.depth_hbm, bf16[2,256,256]{2,1,0:T(8,128)(2,1)} %constant.5.clone.across_hbm, f32[3,64]{1,0:T(4,128)} %color_hbm.1, f32[64]{0:T(128)} %extinction_hbm.1, s32[16]{0:T(128)} %index_hbm.1), custom_call_target="tpu_custom_call" | custom-call | tf_op jit(solution)/shard_map/pallas_call | solution.py:423
  18.7 0.6 %copy.8 = f32[4,1,4,128]{3,2,1,0:T(4,128)} copy(f32[4,1,4,128]{3,2,1,0:T(4,128)S(1)} %shard_map.64) | data formatting | bytes 16384
